TPU v7x, 128 devices: a whole 4x4x4 slice. The times are simulated.
128 devices in a mesh: space: 64 (over x, y, z), sub: 2 (over core).
Axes of the slice: x: 4, y: 4, z: 4, core: 2. Of those that a mesh axis runs over, the one named last changes fastest.
Arguments:
- mode_rows: float32 [256, 1048576], P(None, ('space', 'sub')), as said below
- snapshots: float32 [3, 64, 1048576], P(None, None, ('space', 'sub')), as said below
- probe_fields: float32 [128, 1048576], P(None, ('space', 'sub')), as said below
- core_factor: float32 [256, 256], replicated, as said below
Outputs:
- new_modes: float32 [256, 1048576], P(None, ('space', 'sub'))
- new_core: float32 [256, 256], replicated
- captured: float32 [3, 256, 320], replicated
Inputs may be any that keep to these rules, and one draw needn't show every extreme that they name: `mode_rows`: rows of full rank, entries of order one. `snapshots`: fields of order one. `probe_fields`: fields of order one. `core_factor`: lower triangular with a positive diagonal.
All inputs are finite; a program needn't handle non-finite values.
Results may differ from a plain program's by a relative error of at most 0.0003.
Values sent between devices are 32-bit elements; how exact they have to be, the bound alone decides.
A program may use at most 128 MiB of HBM per device.

v0:
```python
import jax
import jax.numpy as jnp
from jax import lax
from jax.sharding import PartitionSpec as P

TURNS = 2
PRECISE = lax.Precision.HIGHEST


def row_inner(left, right):
    return lax.dot_general(left, right, (((1,), (1,)), ((), ())), precision=PRECISE)


def matmul_high(left, right):
    return jnp.dot(left, right, precision=PRECISE)


def block_cholesky(matrix):
    order = matrix.shape[0]
    width = 64
    lowered = jnp.zeros((order, order), jnp.float32)
    for start in range(0, order, width):
        finish = start + width
        done_rows = lowered[start:finish, :start]
        diag_block = matrix[start:finish, start:finish] - matmul_high(done_rows, done_rows.T)
        diag_factor = jnp.linalg.cholesky(diag_block)
        lowered = lowered.at[start:finish, start:finish].set(diag_factor)
        if finish < order:
            below = matrix[finish:, start:finish] - matmul_high(
                lowered[finish:, :start], done_rows.T
            )
            panel = jax.scipy.linalg.solve_triangular(diag_factor, below.T, lower=True).T
            lowered = lowered.at[finish:, start:finish].set(panel)
    return lowered


def update_core(core_now, projected, factor, turn_count):
    rank_count = core_now.shape[0]
    batch_count = factor.shape[0]
    upper = jnp.concatenate([core_now, projected], axis=1)
    bottom = jnp.concatenate([jnp.zeros((batch_count, rank_count), jnp.float32), factor.T], axis=1)
    stacked = jnp.concatenate([upper, bottom], axis=0)
    squared = matmul_high(stacked, stacked.T)
    rotation = jnp.eye(rank_count + batch_count, rank_count, dtype=jnp.float32)
    for sweep_index in range(turn_count):
        rotation = matmul_high(squared, rotation)
        lowered = block_cholesky(matmul_high(rotation.T, rotation))
        rotation = jax.scipy.linalg.solve_triangular(lowered, rotation.T, lower=True).T
    fresh_core = block_cholesky(matmul_high(rotation.T, matmul_high(squared, rotation)))
    return (rotation, fresh_core)


def orthonormalize(residual, volume):
    gram_local = row_inner(residual, residual)
    factor = block_cholesky(lax.psum(gram_local, ("space", "sub")) * volume)
    orthogonal = jax.scipy.linalg.solve_triangular(factor, residual, lower=True)
    return (factor, orthogonal)


def body(mode_rows, snapshots, probe_fields, core_factor):
    local_rows = mode_rows.shape[1]
    batch_count = snapshots.shape[0]
    batch_width = snapshots.shape[1]
    volume = 1.0 / (local_rows * lax.axis_size("space") * lax.axis_size("sub"))
    window = jnp.concatenate(
        [snapshots.reshape(batch_count * batch_width, local_rows), probe_fields], axis=0
    )
    basis_now = mode_rows
    core_now = core_factor
    captured = []
    for batch_index in range(batch_count):
        incoming = snapshots[batch_index]
        projected = lax.psum(row_inner(basis_now, incoming), ("space", "sub")) * volume
        residual = incoming - matmul_high(projected.T, basis_now)
        factor, orthogonal = orthonormalize(residual, volume)
        rotation, core_now = update_core(core_now, projected, factor, TURNS)
        basis_now = matmul_high(rotation.T, jnp.concatenate([basis_now, orthogonal], axis=0))
        captured.append(lax.psum(row_inner(basis_now, window), ("space", "sub")) * volume)
    return (basis_now, core_now, jnp.stack(captured))


def solution(mesh):
    return jax.shard_map(
        body,
        mesh=mesh,
        in_specs=(
            P(None, ("space", "sub")),
            P(None, None, ("space", "sub")),
            P(None, ("space", "sub")),
            P(),
        ),
        out_specs=(P(None, ("space", "sub")), P(), P()),
        check_vma=False,
    )
```

profile of v0, /device:TPU:1, one launch (start us, length us, event | category | flops | bytes accessed | tf_op | source)
XLA Modules:
  0.0 1623.2 jit_solution(15675498892306487198)
XLA Ops:
  7.2 10.0 fusion.19
  17.3 143.2 %all-reduce.18.cloned.1.call-done = f32[256,64]{1,0:T(8,128)} async-done(((f32[256,64]{1,0:T(8,128)}), f32[256,64]{1,0:T(8,128)}) %all-reduce.18.cloned.1.call-update) | async-done | bytes 65552 | tf_op jit(solution)/shard_map/psum | solution.py:73
  160.5 9.2 convolution_subtract_fusion.2
  171.5 63.6 %psum.64 = f32[64,64]{0,1:T(8,128)S(1)} all-reduce(f32[64,64]{0,1:T(8,128)S(1)} %fusion.442), channel_id=1, replica_groups=mesh['space'=64,'sub'=2] {'space','sub'}, use_global_device_ids=true, to_apply=%region_1.0 | all-reduce | flops 4096 | bytes 32768 | tf_op jit(solution)/shard_map/psum | solution.py:55
  245.5 5.8 cholesky.610
  308.2 20.1 %custom-call.51 = f32[2,128,128]{1,2,0:T(8,128)S(1)} custom-call(f32[2,128,128]{2,1,0:T(8,128)S(1)} %get-tuple-element.863), custom_call_target="InvertDiagBlocksLowerTriangular" | custom-call | tf_op jit(solution)/shard_map/jit(_solve_triangular)/triangular_solve | solution.py:48
  330.9 5.8 cholesky.654
  398.1 19.8 %custom-call.55 = f32[2,128,128]{1,2,0:T(8,128)S(1)} custom-call(f32[2,128,128]{2,1,0:T(8,128)S(1)} %get-tuple-element.864), custom_call_target="InvertDiagBlocksLowerTriangular" | custom-call | tf_op jit(solution)/shard_map/jit(_solve_triangular)/triangular_solve | solution.py:48
  420.5 5.8 cholesky.698
  480.7 16.3 %fusion = f32[256,8192]{1,0:T(8,128)S(1)} fusion(f32[64,8192]{1,0:T(8,128)} %fusion.189, f32[256,8192]{1,0:T(8,128)} %param.153, f32[128,320]{0,1:T(8,128)S(1)} %fusion.125, f32[128,320]{0,1:T(8,128)S(1)} %fusion.98), kind=kOutput, calls=%fused_computation.12 | convolution fusion | flops 8055767040 | bytes 19202048 | tf_op jit(solution)/shard_map/dot_general | solution.py:15
  500.4 8.9 fusion.17
  509.3 13.3 fusion.14
  524.3 122.0 %all-reduce.20.cloned.1.call-done = f32[256,64]{1,0:T(8,128)} async-done(((f32[256,64]{1,0:T(8,128)}), f32[256,64]{1,0:T(8,128)}) %all-reduce.20.cloned.1.call-update) | async-done | bytes 65552 | tf_op jit(solution)/shard_map/psum | solution.py:73
  646.3 9.2 convolution_subtract_fusion.1
  657.2 63.7 %psum.66 = f32[64,64]{0,1:T(8,128)S(1)} all-reduce(f32[64,64]{0,1:T(8,128)S(1)} %fusion.445), channel_id=1, replica_groups=mesh['space'=64,'sub'=2] {'space','sub'}, use_global_device_ids=true, to_apply=%region_5.12 | all-reduce | flops 4096 | bytes 32768 | tf_op jit(solution)/shard_map/psum | solution.py:55
  731.3 5.8 cholesky.753
  794.5 19.8 %custom-call.63 = f32[2,128,128]{1,2,0:T(8,128)S(1)} custom-call(f32[2,128,128]{2,1,0:T(8,128)S(1)} %get-tuple-element.865), custom_call_target="InvertDiagBlocksLowerTriangular" | custom-call | tf_op jit(solution)/shard_map/jit(_solve_triangular)/triangular_solve | solution.py:48
  816.9 5.8 cholesky.797
  884.3 19.9 %custom-call.67 = f32[2,128,128]{1,2,0:T(8,128)S(1)} custom-call(f32[2,128,128]{2,1,0:T(8,128)S(1)} %get-tuple-element.866), custom_call_target="InvertDiagBlocksLowerTriangular" | custom-call | tf_op jit(solution)/shard_map/jit(_solve_triangular)/triangular_solve | solution.py:48
  906.7 5.8 cholesky.841
  944.9 17.2 %fusion.4 = f32[256,8192]{1,0:T(8,128)S(1)} fusion(f32[64,8192]{1,0:T(8,128)S(1)} %fusion.165, f32[256,8192]{1,0:T(8,128)} %copy-done.1, f32[128,320]{0,1:T(8,128)S(1)} %fusion.115, f32[128,320]{0,1:T(8,128)S(1)} %fusion.94), kind=kOutput, calls=%fused_computation.16 | convolution fusion | flops 8055767040 | bytes 19202048 | tf_op jit(solution)/shard_map/dot_general | solution.py:15
  965.3 8.9 fusion.15
  974.2 13.1 fusion.13
  1010.1 114.5 %all-reduce.22.cloned.1.call-done = f32[256,64]{1,0:T(8,128)} async-done(((f32[256,64]{1,0:T(8,128)}), f32[256,64]{1,0:T(8,128)}) %all-reduce.22.cloned.1.call-update) | async-done | bytes 65552 | tf_op jit(solution)/shard_map/psum | solution.py:73
  1124.6 9.2 convolution_subtract_fusion
  1135.6 63.8 %psum.68 = f32[64,64]{0,1:T(8,128)S(1)} all-reduce(f32[64,64]{0,1:T(8,128)S(1)} %fusion.448), channel_id=1, replica_groups=mesh['space'=64,'sub'=2] {'space','sub'}, use_global_device_ids=true, to_apply=%region_7.14 | all-reduce | flops 4096 | bytes 32768 | tf_op jit(solution)/shard_map/psum | solution.py:55
  1272.4 19.9 %custom-call.75 = f32[2,128,128]{1,2,0:T(8,128)S(1)} custom-call(f32[2,128,128]{2,1,0:T(8,128)S(1)} %get-tuple-element.867), custom_call_target="InvertDiagBlocksLowerTriangular" | custom-call | tf_op jit(solution)/shard_map/jit(_solve_triangular)/triangular_solve | solution.py:48
  1362.3 20.1 %custom-call.79 = f32[2,128,128]{1,2,0:T(8,128)S(1)} custom-call(f32[2,128,128]{2,1,0:T(8,128)S(1)} %get-tuple-element.868), custom_call_target="InvertDiagBlocksLowerTriangular" | custom-call | tf_op jit(solution)/shard_map/jit(_solve_triangular)/triangular_solve | solution.py:48
  1384.9 5.8 cholesky.984
  1422.8 18.3 %fusion.8 = f32[256,8192]{1,0:T(8,128)} fusion(f32[64,8192]{1,0:T(8,128)S(1)} %fusion.148, f32[256,8192]{1,0:T(8,128)} %copy-done, f32[128,320]{0,1:T(8,128)S(1)} %fusion.105, f32[128,320]{0,1:T(8,128)S(1)} %fusion.90), kind=kOutput, calls=%fused_computation.20 | convolution fusion | flops 8055767040 | bytes 19202048 | tf_op jit(solution)/shard_map/dot_general | solution.py:15
  1455.7 13.1 fusion.12
  1477.1 136.2 %all-reduce.24.cloned.1.call-done = (f32[256,320]{0,1:T(8,128)}, f32[256,320]{0,1:T(8,128)}, f32[256,320]{0,1:T(8,128)}) async-done(((f32[256,320]{0,1:T(8,128)}, f32[256,320]{0,1:T(8,128)}, f32[256,320]{0,1:T(8,128)}), (f32[256,320]{0,1:T(8,128)}, f32[256,320]{0,1:T(8,128)}, f32[256,320]{0,1:T(8,128)})) %all-reduce.24.cloned.1.call-update) | async-done | bytes 983056 | tf_op jit(solution)/shard_map/psum | solution.py:78
  (551 shorter events, 616.1 us)
Async XLA Ops:
  7.2 153.3 %all-reduce.18.cloned.1.call-start = ((), (), s32[]{:S(2)}) async-start(), calls=%async_computation | async-start | bytes 262144 | tf_op jit(solution)/shard_map/psum | solution.py:73
  17.2 629.1 %all-reduce.20.cloned.1.call-start = ((), (), s32[]{:S(2)}) async-start(), calls=%async_computation.1 | async-start | bytes 262144 | tf_op jit(solution)/shard_map/psum | solution.py:73
  17.3 225.8 %copy-start.9 = (f32[256,256]{1,0:T(8,128)S(1)}, f32[256,256]{1,0:T(8,128)}, u32[]{:S(2)}) copy-start(f32[256,256]{1,0:T(8,128)} %param.156) | copy-start | bytes 786436
  160.5 82.5 %copy-start.6 = (f32[256,64]{1,0:T(8,128)S(1)}, f32[256,64]{1,0:T(8,128)}, u32[]{:S(2)}) copy-start(f32[256,64]{1,0:T(8,128)} %all-reduce.18.cloned.1.call-done) | copy-start | bytes 196612
  245.4 34.5 %copy-start.2 = (f32[256,256]{0,1:T(8,128)}, f32[256,256]{0,1:T(8,128)S(1)}, u32[]{:S(2)}) copy-start(f32[256,256]{0,1:T(8,128)S(1)} %fusion.443) | copy-start | bytes 786436
  497.0 3.4 copy-start.1
  509.3 615.3 %all-reduce.22.cloned.1.call-start = ((), (), s32[]{:S(2)}) async-start(), calls=%async_computation.2 | async-start | bytes 262144 | tf_op jit(solution)/shard_map/psum | solution.py:73
  646.3 82.6 %copy-start.7 = (f32[256,64]{1,0:T(8,128)S(1)}, f32[256,64]{1,0:T(8,128)}, u32[]{:S(2)}) copy-start(f32[256,64]{1,0:T(8,128)} %all-reduce.20.cloned.1.call-done) | copy-start | bytes 196612
  731.2 34.8 %copy-start.3 = (f32[256,256]{0,1:T(8,128)}, f32[256,256]{0,1:T(8,128)S(1)}, u32[]{:S(2)}) copy-start(f32[256,256]{0,1:T(8,128)S(1)} %fusion.446) | copy-start | bytes 786436
  962.1 3.2 copy-start
  987.3 626.0 %all-reduce.24.cloned.1.call-start = ((), (), s32[]{:S(2)}) async-start(), calls=%async_computation.3 | async-start | bytes 1966080 | tf_op jit(solution)/shard_map/psum | solution.py:78
  1124.6 82.8 %copy-start.5 = (f32[256,64]{1,0:T(8,128)S(1)}, f32[256,64]{1,0:T(8,128)}, u32[]{:S(2)}) copy-start(f32[256,64]{1,0:T(8,128)} %all-reduce.22.cloned.1.call-done) | copy-start | bytes 196612
  1209.7 34.4 %copy-start.4 = (f32[256,256]{0,1:T(8,128)}, f32[256,256]{0,1:T(8,128)S(1)}, u32[]{:S(2)}) copy-start(f32[256,256]{0,1:T(8,128)S(1)} %fusion.449) | copy-start | bytes 786436
  1477.0 139.4 %copy-start.8 = (f32[256,256]{1,0:T(8,128)}, f32[256,256]{1,0:T(8,128)S(1)}, u32[]{:S(2)}) copy-start(f32[256,256]{1,0:T(8,128)S(1)} %scatter.314) | copy-start | bytes 786436
Sparse Core Ops, SparseCore 0:
  17.3 143.1 all-reduce.17
  509.4 136.8 all-reduce.19
  987.5 137.0 all-reduce.21
  1469.0 144.2 all-reduce.23
where the time goes:
time: 1630 us; the launch traced here: 1620 us
  other arithmetic  568 us (35%)
  waiting for transfers between devices  516 us (32%)
  matrix products  212 us (13%)
  blocking collectives  191 us (12%)
  local copies, waits for them, and re-layouts  118 us (7%)
  between operations  16.6 us (1%)
    psum x3, waiting for transfers between devices, body(): lax.psum(row_inner(basis_now, incoming), ('space', 'sub')) * volume  380 us
    another operation x117, other arithmetic, block_cholesky(): diag_factor = jnp.linalg.cholesky(diag_block)  255 us
    psum x3, blocking collectives, orthonormalize(): factor = block_cholesky(lax.psum(gram_local, ('space', 'sub')) * volume)  191 us
    another operation x54, other arithmetic, block_cholesky(): jax.scipy.linalg.solve_triangular(diag_factor, below.T, lower=True)  161 us
    psum x1, waiting for transfers between devices, body(): lax.psum(row_inner(basis_now, window), ('space', 'sub')) * volume  136 us
    another operation x13, other arithmetic, update_core(): jax.scipy.linalg.solve_triangular(lowered, rotation.T, lower=True)  123 us
    dot_general x72, matrix products, matmul_high(): return jnp.dot(left, right, precision=PRECISE)  114 us
    dot_general x9, matrix products, row_inner(): lax.dot_general(left, right, (((1,), (1,)), ((), ())), precision=PRECISE)  72.7 us
  transfers between devices with their start and end apart: 4, of which 4 were waited for; matrix products, arithmetic and copies ran while one was open for 3% of the time, Pallas kernels for 0%

commit v1 on v0

--- a/solution.py
+++ b/solution.py
@@ -70,7 +70,7 @@
     captured = []
     for batch_index in range(batch_count):
         incoming = snapshots[batch_index]
-        projected = lax.psum(row_inner(basis_now, incoming), ("space", "sub")) * volume
+        projected = lax.psum(lax.psum(row_inner(basis_now, incoming), "space"), "sub") * volume
         residual = incoming - matmul_high(projected.T, basis_now)
         factor, orthogonal = orthonormalize(residual, volume)
         rotation, core_now = update_core(core_now, projected, factor, TURNS)

time: 1630 us -> 1660 us (1.018)
  waiting for transfers between devices: 516 us -> 536 us
    psum x3 -> x6, waiting for transfers between devices: 380 us -> 400 us  [the longest x3 325 us: body(): lax.psum(row_inner(basis_now, incoming), 'space')]
  transfers between devices with their start and end apart: 4 -> 7, of which waited for: 4 -> 7; matrix products, arithmetic and copies ran while one was open for 3% -> 3% of each run, Pallas kernels for 0% -> 0%
where the time goes in v1:
time: 1660 us; the launch traced here: 1650 us
  other arithmetic  568 us (34%)
  waiting for transfers between devices  536 us (32%)
  matrix products  212 us (13%)
  blocking collectives  201 us (12%)
  local copies, waits for them, and re-layouts  119 us (7%)
  between operations  16.9 us (1%)
    psum x3, waiting for transfers between devices, body(): lax.psum(row_inner(basis_now, incoming), 'space')  325 us
    another operation x117, other arithmetic, block_cholesky(): diag_factor = jnp.linalg.cholesky(diag_block)  255 us
    psum x3, blocking collectives, orthonormalize(): factor = block_cholesky(lax.psum(gram_local, ('space', 'sub')) * volume)  201 us
    another operation x54, other arithmetic, block_cholesky(): jax.scipy.linalg.solve_triangular(diag_factor, below.T, lower=True)  161 us
    psum x1, waiting for transfers between devices, body(): lax.psum(row_inner(basis_now, window), ('space', 'sub')) * volume  136 us
    another operation x13, other arithmetic, update_core(): jax.scipy.linalg.solve_triangular(lowered, rotation.T, lower=True)  123 us
    dot_general x72, matrix products, matmul_high(): return jnp.dot(left, right, precision=PRECISE)  114 us
    psum x3, waiting for transfers between devices, body(): lax.psum(lax.psum(row_inner(basis_now, incoming), 'space'), 'sub') * volume  74.8 us
  transfers between devices with their start and end apart: 7, of which 7 were waited for; matrix products, arithmetic and copies ran while one was open for 3% of the time, Pallas kernels for 0%

profile of v1, /device:TPU:1, one launch (start us, length us, event | category | flops | bytes accessed | tf_op | source)
XLA Modules:
  0.0 1653.4 jit_solution(10292930476754275377)
XLA Ops:
  7.2 10.0 fusion.19
  17.2 124.4 %all-reduce.21.cloned.1.call-done = f32[256,64]{1,0:T(8,128)} async-done(((f32[256,64]{1,0:T(8,128)}), f32[256,64]{1,0:T(8,128)}) %all-reduce.21.cloned.1.call-update) | async-done | bytes 65552 | tf_op jit(solution)/shard_map/psum | solution.py:73
  141.8 26.2 %all-reduce.23.cloned.1.call-done = f32[256,64]{1,0:T(8,128)} async-done(((f32[256,64]{1,0:T(8,128)}), f32[256,64]{1,0:T(8,128)}) %all-reduce.23.cloned.1.call-update) | async-done | bytes 65552 | tf_op jit(solution)/shard_map/psum | solution.py:73
  167.9 9.2 convolution_subtract_fusion.2
  178.9 66.9 %psum.86 = f32[64,64]{0,1:T(8,128)S(1)} all-reduce(f32[64,64]{0,1:T(8,128)S(1)} %fusion.442), channel_id=1, replica_groups=mesh['space'=64,'sub'=2] {'space','sub'}, use_global_device_ids=true, to_apply=%region_2.0 | all-reduce | flops 4096 | bytes 32768 | tf_op jit(solution)/shard_map/psum | solution.py:55
  256.2 5.8 cholesky.610
  319.0 20.1 %custom-call.51 = f32[2,128,128]{1,2,0:T(8,128)S(1)} custom-call(f32[2,128,128]{2,1,0:T(8,128)S(1)} %get-tuple-element.863), custom_call_target="InvertDiagBlocksLowerTriangular" | custom-call | tf_op jit(solution)/shard_map/jit(_solve_triangular)/triangular_solve | solution.py:48
  341.6 5.8 cholesky.654
  408.8 19.8 %custom-call.55 = f32[2,128,128]{1,2,0:T(8,128)S(1)} custom-call(f32[2,128,128]{2,1,0:T(8,128)S(1)} %get-tuple-element.864), custom_call_target="InvertDiagBlocksLowerTriangular" | custom-call | tf_op jit(solution)/shard_map/jit(_solve_triangular)/triangular_solve | solution.py:48
  431.2 5.8 cholesky.698
  490.7 16.3 fusion
  510.4 8.9 fusion.17
  519.4 13.1 fusion.14
  533.2 103.9 %all-reduce.25.cloned.1.call-done = f32[256,64]{1,0:T(8,128)} async-done(((f32[256,64]{1,0:T(8,128)}), f32[256,64]{1,0:T(8,128)}) %all-reduce.25.cloned.1.call-update) | async-done | bytes 65552 | tf_op jit(solution)/shard_map/psum | solution.py:73
  639.0 24.1 %all-reduce.27.cloned.1.call-done = f32[256,64]{1,0:T(8,128)} async-done(((f32[256,64]{1,0:T(8,128)}), f32[256,64]{1,0:T(8,128)}) %all-reduce.27.cloned.1.call-update) | async-done | bytes 65552 | tf_op jit(solution)/shard_map/psum | solution.py:73
  663.1 9.2 convolution_subtract_fusion.1
  674.1 66.9 %psum.89 = f32[64,64]{0,1:T(8,128)S(1)} all-reduce(f32[64,64]{0,1:T(8,128)S(1)} %fusion.445), channel_id=1, replica_groups=mesh['space'=64,'sub'=2] {'space','sub'}, use_global_device_ids=true, to_apply=%region_7.14 | all-reduce | flops 4096 | bytes 32768 | tf_op jit(solution)/shard_map/psum | solution.py:55
  751.4 5.8 cholesky.753
  814.5 20.1 %custom-call.63 = f32[2,128,128]{1,2,0:T(8,128)S(1)} custom-call(f32[2,128,128]{2,1,0:T(8,128)S(1)} %get-tuple-element.865), custom_call_target="InvertDiagBlocksLowerTriangular" | custom-call | tf_op jit(solution)/shard_map/jit(_solve_triangular)/triangular_solve | solution.py:48
  904.6 19.8 %custom-call.67 = f32[2,128,128]{1,2,0:T(8,128)S(1)} custom-call(f32[2,128,128]{2,1,0:T(8,128)S(1)} %get-tuple-element.866), custom_call_target="InvertDiagBlocksLowerTriangular" | custom-call | tf_op jit(solution)/shard_map/jit(_solve_triangular)/triangular_solve | solution.py:48
  964.9 17.4 %fusion.4 = f32[256,8192]{1,0:T(8,128)S(1)} fusion(f32[64,8192]{1,0:T(8,128)S(1)} %fusion.165, f32[256,8192]{1,0:T(8,128)} %copy-done.1, f32[128,320]{0,1:T(8,128)S(1)} %fusion.115, f32[128,320]{0,1:T(8,128)S(1)} %fusion.94), kind=kOutput, calls=%fused_computation.16 | convolution fusion | flops 8055767040 | bytes 19202048 | tf_op jit(solution)/shard_map/dot_general | solution.py:15
  985.5 8.9 fusion.15
  994.5 13.1 fusion.13
  1028.7 96.8 %all-reduce.29.cloned.1.call-done = f32[256,64]{1,0:T(8,128)} async-done(((f32[256,64]{1,0:T(8,128)}), f32[256,64]{1,0:T(8,128)}) %all-reduce.29.cloned.1.call-update) | async-done | bytes 65552 | tf_op jit(solution)/shard_map/psum | solution.py:73
  1127.3 24.4 %all-reduce.31.cloned.1.call-done = f32[256,64]{1,0:T(8,128)} async-done(((f32[256,64]{1,0:T(8,128)}), f32[256,64]{1,0:T(8,128)}) %all-reduce.31.cloned.1.call-update) | async-done | bytes 65552 | tf_op jit(solution)/shard_map/psum | solution.py:73
  1151.7 9.2 convolution_subtract_fusion
  1162.7 66.9 %psum.92 = f32[64,64]{0,1:T(8,128)S(1)} all-reduce(f32[64,64]{0,1:T(8,128)S(1)} %fusion.448), channel_id=1, replica_groups=mesh['space'=64,'sub'=2] {'space','sub'}, use_global_device_ids=true, to_apply=%region_10.17 | all-reduce | flops 4096 | bytes 32768 | tf_op jit(solution)/shard_map/psum | solution.py:55
  1302.9 19.8 %custom-call.75 = f32[2,128,128]{1,2,0:T(8,128)S(1)} custom-call(f32[2,128,128]{2,1,0:T(8,128)S(1)} %get-tuple-element.867), custom_call_target="InvertDiagBlocksLowerTriangular" | custom-call | tf_op jit(solution)/shard_map/jit(_solve_triangular)/triangular_solve | solution.py:48
  1392.7 19.9 %custom-call.79 = f32[2,128,128]{1,2,0:T(8,128)S(1)} custom-call(f32[2,128,128]{2,1,0:T(8,128)S(1)} %get-tuple-element.868), custom_call_target="InvertDiagBlocksLowerTriangular" | custom-call | tf_op jit(solution)/shard_map/jit(_solve_triangular)/triangular_solve | solution.py:48
  1453.3 18.3 %fusion.8 = f32[256,8192]{1,0:T(8,128)} fusion(f32[64,8192]{1,0:T(8,128)S(1)} %fusion.148, f32[256,8192]{1,0:T(8,128)} %copy-done, f32[128,320]{0,1:T(8,128)S(1)} %fusion.105, f32[128,320]{0,1:T(8,128)S(1)} %fusion.90), kind=kOutput, calls=%fused_computation.20 | convolution fusion | flops 8055767040 | bytes 19202048 | tf_op jit(solution)/shard_map/dot_general | solution.py:15
  1486.1 13.1 fusion.12
  1507.5 135.8 %all-reduce.33.cloned.1.call-done = (f32[256,320]{0,1:T(8,128)}, f32[256,320]{0,1:T(8,128)}, f32[256,320]{0,1:T(8,128)}) async-done(((f32[256,320]{0,1:T(8,128)}, f32[256,320]{0,1:T(8,128)}, f32[256,320]{0,1:T(8,128)}), (f32[256,320]{0,1:T(8,128)}, f32[256,320]{0,1:T(8,128)}, f32[256,320]{0,1:T(8,128)})) %all-reduce.33.cloned.1.call-update) | async-done | bytes 983056 | tf_op jit(solution)/shard_map/psum | solution.py:78
  (560 shorter events, 634.0 us)
Async XLA Ops:
  7.2 134.5 %all-reduce.21.cloned.1.call-start = ((), (), s32[]{:S(2)}) async-start(), calls=%async_computation | async-start | bytes 262144 | tf_op jit(solution)/shard_map/psum | solution.py:73
  17.2 150.8 %all-reduce.23.cloned.1.call-start = ((), (), s32[]{:S(2)}) async-start(), calls=%async_computation.1 | async-start | bytes 262144 | tf_op jit(solution)/shard_map/psum | solution.py:73
  141.7 495.4 %all-reduce.25.cloned.1.call-start = ((), (), s32[]{:S(2)}) async-start(), calls=%async_computation.2 | async-start | bytes 262144 | tf_op jit(solution)/shard_map/psum | solution.py:73
  141.7 112.0 %copy-start.9 = (f32[256,256]{1,0:T(8,128)S(1)}, f32[256,256]{1,0:T(8,128)}, u32[]{:S(2)}) copy-start(f32[256,256]{1,0:T(8,128)} %param.156) | copy-start | bytes 786436
  167.9 85.8 %copy-start.7 = (f32[256,64]{1,0:T(8,128)S(1)}, f32[256,64]{1,0:T(8,128)}, u32[]{:S(2)}) copy-start(f32[256,64]{1,0:T(8,128)} %all-reduce.23.cloned.1.call-done) | copy-start | bytes 196612
  256.1 34.5 %copy-start.2 = (f32[256,256]{0,1:T(8,128)}, f32[256,256]{0,1:T(8,128)S(1)}, u32[]{:S(2)}) copy-start(f32[256,256]{0,1:T(8,128)S(1)} %fusion.443) | copy-start | bytes 786436
  507.0 3.4 copy-start.1
  519.4 143.8 %all-reduce.27.cloned.1.call-start = ((), (), s32[]{:S(2)}) async-start(), calls=%async_computation.3 | async-start | bytes 262144 | tf_op jit(solution)/shard_map/psum | solution.py:73
  637.1 488.4 %all-reduce.29.cloned.1.call-start = ((), (), s32[]{:S(2)}) async-start(), calls=%async_computation.4 | async-start | bytes 262144 | tf_op jit(solution)/shard_map/psum | solution.py:73
  663.1 85.8 %copy-start.5 = (f32[256,64]{1,0:T(8,128)S(1)}, f32[256,64]{1,0:T(8,128)}, u32[]{:S(2)}) copy-start(f32[256,64]{1,0:T(8,128)} %all-reduce.27.cloned.1.call-done) | copy-start | bytes 196612
  751.3 34.7 %copy-start.3 = (f32[256,256]{0,1:T(8,128)}, f32[256,256]{0,1:T(8,128)S(1)}, u32[]{:S(2)}) copy-start(f32[256,256]{0,1:T(8,128)S(1)} %fusion.446) | copy-start | bytes 786436
  982.3 3.2 copy-start
  1007.6 144.1 %all-reduce.31.cloned.1.call-start = ((), (), s32[]{:S(2)}) async-start(), calls=%async_computation.5 | async-start | bytes 262144 | tf_op jit(solution)/shard_map/psum | solution.py:73
  1125.6 517.7 %all-reduce.33.cloned.1.call-start = ((), (), s32[]{:S(2)}) async-start(), calls=%async_computation.6 | async-start | bytes 1966080 | tf_op jit(solution)/shard_map/psum | solution.py:78
  1151.7 85.8 %copy-start.6 = (f32[256,64]{1,0:T(8,128)S(1)}, f32[256,64]{1,0:T(8,128)}, u32[]{:S(2)}) copy-start(f32[256,64]{1,0:T(8,128)} %all-reduce.31.cloned.1.call-done) | copy-start | bytes 196612
  1239.9 34.6 %copy-start.4 = (f32[256,256]{0,1:T(8,128)}, f32[256,256]{0,1:T(8,128)S(1)}, u32[]{:S(2)}) copy-start(f32[256,256]{0,1:T(8,128)S(1)} %fusion.449) | copy-start | bytes 786436
  1507.4 138.9 %copy-start.8 = (f32[256,256]{1,0:T(8,128)}, f32[256,256]{1,0:T(8,128)S(1)}, u32[]{:S(2)}) copy-start(f32[256,256]{1,0:T(8,128)S(1)} %scatter.314) | copy-start | bytes 786436
Sparse Core Ops, SparseCore 0:
  17.3 124.3 all-reduce.20
  144.2 23.6 all-reduce.22
  519.5 117.5 all-reduce.24
  639.4 23.7 all-reduce.26
  1007.7 117.7 all-reduce.28
  1128.0 23.6 all-reduce.30
  1499.4 143.8 all-reduce.32
